TPU v7x, 32 devices: a whole 2x2x4 slice. The times are simulated.
32 devices in a mesh: dp: 16 (over z, y, x), mp: 2 (over core).
Axes of the slice: x: 2, y: 2, z: 4, core: 2. Of those that a mesh axis runs over, the one named last changes fastest.
Arguments:
- gradients: float32 [16, 4, 32, 8192], P('dp', None, 'mp'), may hold values from -6 to 6
- weights: float32 [4, 32, 8192], P(None, 'mp', 'dp'), may hold values from -40 to 40
- first_moment: float32 [4, 32, 8192], P(None, 'mp', 'dp'), may hold values from -0.6 to 0.6
- second_moment: float32 [4, 32, 8192], P(None, 'mp', 'dp'), may hold values from 0.001 to 0.1
- learn_rate: float32 [4], replicated, may hold values from 0.1 to 0.5
- weight_decay: float32 [4], replicated, may hold values from 0.1 to 1
Outputs:
- new_weights: float32 [4, 32, 8192], P(None, 'mp')
- new_first: float32 [4, 32, 8192], P(None, 'mp', 'dp')
- new_second: float32 [4, 32, 8192], P(None, 'mp', 'dp')
- trust_ratio: float32 [4], replicated
All inputs are finite; a program needn't handle non-finite values.
Results may differ from a plain program's by a relative error of at most 0.000062.
Values sent between devices are 32-bit elements; how exact they have to be, the bound alone decides.
No kernel may reach another device: no remote copies, remote signals or barrier semaphores. Data moves between devices by JAX's collectives and lax.ppermute only.
A program may use at most 64 MiB of HBM per device.

v0:
```python
import jax
import jax.numpy as jnp
from jax import lax
from jax.sharding import PartitionSpec as P

STEP = 10


def shards(gradients, weights, first_moment, second_moment, learn_rate, weight_decay):
    replicas = lax.axis_size("dp")
    summed = lax.psum_scatter(gradients, "dp", scatter_dimension=3, tiled=True)[0] * (
        1.0 / replicas
    )
    new_first = 0.9 * first_moment + 0.1 * summed
    new_second = 0.999 * second_moment + 0.001 * summed * summed
    first_fix = 1.0 - 0.9**STEP
    second_fix = 1.0 - 0.999**STEP
    update = (
        new_first / first_fix / (jnp.sqrt(new_second / second_fix) + 1e-06)
        + weight_decay[:, None, None] * weights
    )
    weight_sq, update_sq = lax.psum(
        (jnp.sum(weights * weights, axis=(1, 2)), jnp.sum(update * update, axis=(1, 2))),
        ("dp", "mp"),
    )
    trust_ratio = jnp.sqrt(weight_sq) / (jnp.sqrt(update_sq) + 1e-06)
    stepped = weights - (learn_rate * trust_ratio)[:, None, None] * update
    new_weights = lax.all_gather(stepped, "dp", axis=2, tiled=True)
    return (new_weights, new_first, new_second, trust_ratio)


def solution(mesh):
    in_specs = (
        P("dp", None, "mp", None),
        P(None, "mp", "dp"),
        P(None, "mp", "dp"),
        P(None, "mp", "dp"),
        P(),
        P(),
    )
    out_specs = (P(None, "mp", None), P(None, "mp", "dp"), P(None, "mp", "dp"), P())
    return jax.shard_map(shards, mesh=mesh, in_specs=in_specs, out_specs=out_specs, check_vma=False)
```

profile of v0, /device:TPU:0, one launch (start us, length us, event | category | flops | bytes accessed | tf_op | source)
XLA Modules:
  0.0 205.5 jit_solution(638651230014546051)
XLA Ops:
  7.2 0.0 copy-start
  7.2 0.0 copy-start.3
  7.2 0.0 copy-start.2
  7.2 0.0 copy-start.1
  7.2 0.0 copy-start.4
  7.2 0.0 reduce-scatter.2.cloned.1.call-start
  7.3 0.7 reduce-scatter.2.cloned.1.call-update
  7.9 0.0 all-gather.2.cloned.1.call-start
  8.0 86.7 %reduce-scatter.2.cloned.1.call-done = f32[1,4,16,512]{3,2,1,0:T(8,128)} async-done(((f32[1,4,16,8192]{3,2,1,0:T(8,128)}), f32[1,4,16,512]{3,2,1,0:T(8,128)}) %reduce-scatter.2.cloned.1.call-update) | async-done | bytes 131088 | tf_op jit(solution)/shard_map/reduce_scatter | solution.py:11
  94.7 0.0 copy-done
  94.7 0.0 copy-done.3
  94.7 0.0 copy-done.2
  94.7 0.0 copy-done.1
  94.7 1.7 multiply_reduce_fusion
  96.4 36.8 %all-reduce = (f32[4]{0:T(128)S(1)}, f32[4]{0:T(128)S(1)}) all-reduce(f32[4]{0:T(128)S(1)} %get-tuple-element.8, f32[4]{0:T(128)S(1)} %get-tuple-element.12), channel_id=1, replica_groups=mesh['dp'=16,'mp'=2] {'dp','mp'}, use_global_device_ids=true, to_apply=%region_4.0 | all-reduce | flops 8 | bytes 64 | tf_op jit(solution)/shard_map/psum | solution.py:22
  133.2 0.0 copy-done.4
  133.2 0.5 fusion
  133.7 0.7 multiply_subtract_fusion
  134.4 0.0 all-gather.2.cloned.1.call-update
  134.5 61.1 %all-gather.2.cloned.1.call-done = f32[4,16,8192]{2,1,0:T(8,128)} async-done(((f32[4,16,512]{2,1,0:T(8,128)}), f32[4,16,8192]{2,1,0:T(8,128)}) %all-gather.2.cloned.1.call-update) | async-done | bytes 2097168 | tf_op jit(solution)/shard_map/all_gather | solution.py:28
  195.6 3.1 %copy.11 = f32[4,16,8192]{2,1,0:T(8,128)} copy(f32[4,16,8192]{2,1,0:T(8,128)} %all-gather.2.cloned.1.call-done) | data formatting | bytes 4194304
Async XLA Ops:
  7.2 87.5 %copy-start = (f32[4,16,512]{2,1,0:T(8,128)S(1)}, f32[4,16,512]{2,1,0:T(8,128)}, u32[]{:S(2)}) copy-start(f32[4,16,512]{2,1,0:T(8,128)} %param.7) | copy-start | bytes 393220
  7.2 87.5 %copy-start.3 = (f32[4]{0:T(128)S(1)}, f32[4]{0:T(128)}, u32[]{:S(2)}) copy-start(f32[4]{0:T(128)} %param.11) | copy-start | bytes 52
  7.2 87.5 %copy-start.2 = (f32[4,16,512]{2,1,0:T(8,128)S(1)}, f32[4,16,512]{2,1,0:T(8,128)}, u32[]{:S(2)}) copy-start(f32[4,16,512]{2,1,0:T(8,128)} %param.9) | copy-start | bytes 393220
  7.2 87.5 %copy-start.1 = (f32[4,16,512]{2,1,0:T(8,128)S(1)}, f32[4,16,512]{2,1,0:T(8,128)}, u32[]{:S(2)}) copy-start(f32[4,16,512]{2,1,0:T(8,128)} %param.8) | copy-start | bytes 393220
  7.2 126.0 %copy-start.4 = (f32[4]{0:T(128)S(1)}, f32[4]{0:T(128)}, u32[]{:S(2)}) copy-start(f32[4]{0:T(128)} %param.10) | copy-start | bytes 52
  7.2 87.4 %reduce-scatter.2.cloned.1.call-start = ((), (), s32[]{:S(2)}) async-start(), calls=%async_computation.1 | async-start | bytes 2228224 | tf_op jit(solution)/shard_map/reduce_scatter | solution.py:11
  7.9 187.6 %all-gather.2.cloned.1.call-start = ((), (), s32[]{:S(2)}) async-start(), calls=%async_computation.2 | async-start | bytes 2228224 | tf_op jit(solution)/shard_map/all_gather | solution.py:28
Sparse Core Ops, SparseCore 0:
  10.3 84.3 reduce-scatter.1
  134.6 60.9 all-gather.1
where the time goes:
time: 206 us; the launch traced here: 205 us
  waiting for transfers between devices  148 us (72%)
  blocking collectives  36.8 us (18%)
  between operations  14.1 us (7%)
  local copies, waits for them, and re-layouts  3.08 us (1%)
  other arithmetic  2.97 us (1%)
    reduce_scatter x1, waiting for transfers between devices, shards(): lax.psum_scatter(gradients, 'dp', scatter_dimension=3, tiled=True)[0]  86.7 us
    all_gather x1, waiting for transfers between devices, shards(): new_weights = lax.all_gather(stepped, 'dp', axis=2, tiled=True)  61.1 us
    psum x1, blocking collectives, shards(): lax.psum((jnp.sum(weights * weights, axis=(1, 2)), jnp.sum(update * updat...  36.8 us
  transfers between devices with their start and end apart: 2, of which 2 were waited for; matrix products, arithmetic and copies ran while one was open for 0% of the time, Pallas kernels for 0%

commit v1 on v0

--- a/solution.py
+++ b/solution.py
@@ -4,6 +4,11 @@
 from jax.sharding import PartitionSpec as P
 
 STEP = 10
+
+
+def one_after_other(x, inner_axis, outer_axis):
+    inner = lax.psum(x, inner_axis)
+    return lax.psum(inner, outer_axis)
 
 
 def shards(gradients, weights, first_moment, second_moment, learn_rate, weight_decay):
@@ -19,9 +24,8 @@
         new_first / first_fix / (jnp.sqrt(new_second / second_fix) + 1e-06)
         + weight_decay[:, None, None] * weights
     )
-    weight_sq, update_sq = lax.psum(
-        (jnp.sum(weights * weights, axis=(1, 2)), jnp.sum(update * update, axis=(1, 2))),
-        ("dp", "mp"),
+    weight_sq, update_sq = one_after_other(
+        (jnp.sum(weights * weights, axis=(1, 2)), jnp.sum(update * update, axis=(1, 2))), "mp", "dp"
     )
     trust_ratio = jnp.sqrt(weight_sq) / (jnp.sqrt(update_sq) + 1e-06)
     stepped = weights - (learn_rate * trust_ratio)[:, None, None] * update

time: 206 us -> 205 us (level)
  waiting for transfers between devices: 148 us -> 145 us
  blocking collectives: 36.8 us -> 39.6 us
    all_gather x1, waiting for transfers between devices: 61.1 us -> 57.9 us  [shards(): new_weights = lax.all_gather(stepped, 'dp', axis=2, tiled=True)]
    psum x1 -> x2, blocking collectives: 36.8 us -> 39.6 us  [the longest x1 37.1 us: one_after_other(): return lax.psum(inner, outer_axis)]
where the time goes in v1:
time: 205 us
  waiting for transfers between devices  145 us (71%)
  blocking collectives  39.6 us (19%)
  between operations  14.1 us (7%)
  local copies, waits for them, and re-layouts  3.08 us (2%)
  other arithmetic  2.97 us (1%)
    reduce_scatter x1, waiting for transfers between devices, shards(): lax.psum_scatter(gradients, 'dp', scatter_dimension=3, tiled=True)[0]  86.7 us
    all_gather x1, waiting for transfers between devices, shards(): new_weights = lax.all_gather(stepped, 'dp', axis=2, tiled=True)  57.9 us
    psum x1, blocking collectives, one_after_other(): return lax.psum(inner, outer_axis)  37.1 us
  transfers between devices with their start and end apart: 2, of which 2 were waited for; matrix products, arithmetic and copies ran while one was open for 0% of the time, Pallas kernels for 0%

profile of v1, /device:TPU:0, one launch (start us, length us, event | category | flops | bytes accessed | tf_op | source)
XLA Modules:
  0.0 205.1 jit_solution(5192132023119095114)
XLA Ops:
  7.2 0.0 copy-start
  7.2 0.0 copy-start.3
  7.2 0.0 copy-start.2
  7.2 0.0 copy-start.1
  7.2 0.0 copy-start.4
  7.2 0.0 reduce-scatter.2.cloned.1.call-start
  7.3 0.7 reduce-scatter.2.cloned.1.call-update
  7.9 0.0 all-gather.2.cloned.1.call-start
  8.0 86.7 %reduce-scatter.2.cloned.1.call-done = f32[1,4,16,512]{3,2,1,0:T(8,128)} async-done(((f32[1,4,16,8192]{3,2,1,0:T(8,128)}), f32[1,4,16,512]{3,2,1,0:T(8,128)}) %reduce-scatter.2.cloned.1.call-update) | async-done | bytes 131088 | tf_op jit(solution)/shard_map/reduce_scatter | solution.py:16
  94.7 0.0 copy-done
  94.7 0.0 copy-done.3
  94.7 0.0 copy-done.2
  94.7 0.0 copy-done.1
  94.7 1.7 multiply_reduce_fusion
  96.4 2.4 %all-reduce.1 = (f32[4]{0:T(128)S(1)}, f32[4]{0:T(128)S(1)}) all-reduce(f32[4]{0:T(128)S(1)} %get-tuple-element.10, f32[4]{0:T(128)S(1)} %get-tuple-element.14), channel_id=1, replica_groups=mesh['dp'=16,'mp'=2] {'mp'}, use_global_device_ids=true, to_apply=%region_5.0 | all-reduce | flops 8 | bytes 64 | tf_op jit(solution)/shard_map/psum | solution.py:10
  98.8 37.1 %all-reduce = (f32[4]{0:T(128)S(1)}, f32[4]{0:T(128)S(1)}) all-reduce(f32[4]{0:T(128)S(1)} %get-tuple-element.6, f32[4]{0:T(128)S(1)} %get-tuple-element.7), channel_id=1, replica_groups=mesh['dp'=16,'mp'=2] {'dp'}, use_global_device_ids=true, to_apply=%region_6.0 | all-reduce | flops 8 | bytes 64 | tf_op jit(solution)/shard_map/psum | solution.py:11
  136.0 0.0 copy-done.4
  136.0 0.5 fusion
  136.5 0.7 multiply_subtract_fusion
  137.2 0.0 all-gather.2.cloned.1.call-update
  137.3 57.9 %all-gather.2.cloned.1.call-done = f32[4,16,8192]{2,1,0:T(8,128)} async-done(((f32[4,16,512]{2,1,0:T(8,128)}), f32[4,16,8192]{2,1,0:T(8,128)}) %all-gather.2.cloned.1.call-update) | async-done | bytes 2097168 | tf_op jit(solution)/shard_map/all_gather | solution.py:32
  195.2 3.1 %copy.11 = f32[4,16,8192]{2,1,0:T(8,128)} copy(f32[4,16,8192]{2,1,0:T(8,128)} %all-gather.2.cloned.1.call-done) | data formatting | bytes 4194304
Async XLA Ops:
  7.2 87.5 %copy-start = (f32[4,16,512]{2,1,0:T(8,128)S(1)}, f32[4,16,512]{2,1,0:T(8,128)}, u32[]{:S(2)}) copy-start(f32[4,16,512]{2,1,0:T(8,128)} %param.7) | copy-start | bytes 393220
  7.2 87.5 %copy-start.3 = (f32[4]{0:T(128)S(1)}, f32[4]{0:T(128)}, u32[]{:S(2)}) copy-start(f32[4]{0:T(128)} %param.11) | copy-start | bytes 52
  7.2 87.5 %copy-start.2 = (f32[4,16,512]{2,1,0:T(8,128)S(1)}, f32[4,16,512]{2,1,0:T(8,128)}, u32[]{:S(2)}) copy-start(f32[4,16,512]{2,1,0:T(8,128)} %param.9) | copy-start | bytes 393220
  7.2 87.5 %copy-start.1 = (f32[4,16,512]{2,1,0:T(8,128)S(1)}, f32[4,16,512]{2,1,0:T(8,128)}, u32[]{:S(2)}) copy-start(f32[4,16,512]{2,1,0:T(8,128)} %param.8) | copy-start | bytes 393220
  7.2 128.8 %copy-start.4 = (f32[4]{0:T(128)S(1)}, f32[4]{0:T(128)}, u32[]{:S(2)}) copy-start(f32[4]{0:T(128)} %param.10) | copy-start | bytes 52
  7.2 87.4 %reduce-scatter.2.cloned.1.call-start = ((), (), s32[]{:S(2)}) async-start(), calls=%async_computation.1 | async-start | bytes 2228224 | tf_op jit(solution)/shard_map/reduce_scatter | solution.py:16
  7.9 187.2 %all-gather.2.cloned.1.call-start = ((), (), s32[]{:S(2)}) async-start(), calls=%async_computation.2 | async-start | bytes 2228224 | tf_op jit(solution)/shard_map/all_gather | solution.py:32
Sparse Core Ops, SparseCore 0:
  10.3 84.3 reduce-scatter.1
  137.4 57.7 all-gather.1
